TPU v7x, 512 devices: a whole 4x4x16 slice. The times are simulated.
512 devices in a mesh: dp: 4 (over y), head: 2 (over core), tile: 64 (over z, x).
Axes of the slice: x: 4, y: 4, z: 16, core: 2. Of those that a mesh axis runs over, the one named last changes fastest.
Arguments:
- tiles_in: bfloat16 [4, 16384, 2560], P('dp', 'tile'), may hold values from -6 to 6
- key_weight: bfloat16 [2560, 1280], P('tile', 'head'), may hold values from -0.125 to 0.125
- value_weight: bfloat16 [2560, 1280], P('tile', 'head'), may hold values from -0.125 to 0.125
- queries: bfloat16 [512, 1280], P(None, 'head'), may hold values from -300 to 300
- out_grad: bfloat16 [4, 512, 1280], P('dp', None, 'head'), may hold values from -1536 to 1536
- valid_count: int32 [4], P('dp'), may hold values from 4096 to 16384, as said below
- tile_mask: int32 [4, 16384], P('dp', 'tile'), may hold values 0 or 1
Outputs:
- tile_grad: bfloat16 [4, 16384, 2560], P('dp', 'tile', 'head')
Inputs may be any that keep to these rules, and one draw needn't show every extreme that they name: Some slide has valid_count equal to 16384.
All inputs are finite; a program needn't handle non-finite values. No bound on the sum of `tile_mask` on one device may be relied on, other than what follows from the above.
Results may differ from a plain program's by a relative error of at most 0.022.
Values may be sent and summed in bfloat16 or wider, within the bound.
No kernel may reach another device: no remote copies, remote signals or barrier semaphores. Data moves between devices by JAX's collectives and lax.ppermute only.
A program may use at most 64 MiB of HBM per device.

v0:
```python
import jax
import jax.numpy as jnp
from jax import lax
from jax.sharding import PartitionSpec as P

HDIM = 80


NEG_LARGE = -1e30


def per_device(tiles_in, key_weight, value_weight, queries, out_grad, valid_count, tile_mask):
    inv_scale = HDIM ** (-0.5)
    tile_dev = tiles_in.shape[1]
    group_width = queries.shape[1]
    heads_here = group_width // HDIM
    latents = queries.shape[0]
    local_tiles = tiles_in[0]
    positions = lax.axis_index("tile") * tile_dev + jnp.arange(tile_dev, dtype=jnp.int32)
    kept = (tile_mask[0] == 1) | (positions == 0)
    valid = ((positions < valid_count[0]) & kept)[None, None, :]
    full_key, full_value = (
        lax.all_gather(key_weight, "tile", axis=0, tiled=True),
        lax.all_gather(value_weight, "tile", axis=0, tiled=True),
    )
    keys = jnp.dot(local_tiles, full_key, preferred_element_type=jnp.float32)
    values = jnp.dot(local_tiles, full_value, preferred_element_type=jnp.float32).astype(
        jnp.bfloat16
    )
    query_heads = queries.reshape(latents, heads_here, HDIM)
    query_wide = queries.astype(jnp.float32).reshape(latents, heads_here, HDIM)
    key_heads = keys.reshape(tile_dev, heads_here, HDIM)
    value_heads = values.reshape(tile_dev, heads_here, HDIM)
    grad_heads = out_grad[0].reshape(latents, heads_here, HDIM)
    scores = (
        jnp.einsum(
            "lhd,thd->hlt",
            query_wide,
            key_heads,
            precision=lax.Precision.HIGHEST,
            preferred_element_type=jnp.float32,
        )
        * inv_scale
    )
    prob_grad = jnp.einsum(
        "lhd,thd->hlt", grad_heads, value_heads, preferred_element_type=jnp.float32
    )
    local_max = jnp.max(jnp.where(valid, scores, NEG_LARGE), axis=2)
    row_max = lax.pmax(local_max, "tile")
    expd = jnp.where(valid, jnp.exp(scores - row_max[:, :, None]), 0.0)
    total, weighted = lax.psum((jnp.sum(expd, axis=2), jnp.sum(expd * prob_grad, axis=2)), "tile")
    delta = weighted / total
    probs = expd / total[:, :, None]
    dscore = (inv_scale * probs * (prob_grad - delta[:, :, None])).astype(jnp.bfloat16)
    value_grad = (
        jnp.einsum(
            "hlt,lhd->thd",
            probs.astype(jnp.bfloat16),
            grad_heads,
            preferred_element_type=jnp.float32,
        )
        .astype(jnp.bfloat16)
        .reshape(tile_dev, group_width)
    )
    key_grad = (
        jnp.einsum("hlt,lhd->thd", dscore, query_heads, preferred_element_type=jnp.float32)
        .astype(jnp.bfloat16)
        .reshape(tile_dev, group_width)
    )
    partial_sum = jnp.einsum("tc,rc->tr", key_grad, full_key, preferred_element_type=jnp.float32)
    partial_sum = partial_sum + jnp.einsum(
        "tc,rc->tr", value_grad, full_value, preferred_element_type=jnp.float32
    )
    rounded = partial_sum.astype(jnp.bfloat16)
    summed = lax.psum_scatter(rounded[None], "head", scatter_dimension=2, tiled=True).astype(
        jnp.float32
    )
    return summed.astype(jnp.bfloat16)


def solution(mesh):
    return jax.shard_map(
        per_device,
        mesh=mesh,
        in_specs=(
            P("dp", "tile", None),
            P("tile", "head"),
            P("tile", "head"),
            P(None, "head"),
            P("dp", None, "head"),
            P("dp"),
            P("dp", "tile"),
        ),
        out_specs=P("dp", "tile", "head"),
        check_vma=False,
    )
```

profile of v0, /device:TPU:1, one launch (start us, length us, event | category | flops | bytes accessed | tf_op | source)
XLA Modules:
  0.0 901.9 jit_solution(17040804668018746320)
XLA Ops:
  6.5 0.0 copy-start
  6.5 0.0 all-gather.5.cloned.1.call-start
  6.5 0.7 all-gather.5.cloned.1.call-update
  7.3 0.0 all-gather.3.cloned.1.call-start
  7.3 0.7 all-gather.3.cloned.1.call-update
  8.0 0.0 reduce-scatter.2.cloned.1.call-start
  8.7 1.3 copy.22
  10.0 1.3 copy.24
  11.4 0.7 compare_reduce_fusion
  12.1 139.2 %all-gather.5.cloned.1.call-done = bf16[2560,640]{1,0:T(8,128)(2,1)} async-done(((bf16[40,640]{1,0:T(8,128)(2,1)}), bf16[2560,640]{1,0:T(8,128)(2,1)}) %all-gather.5.cloned.1.call-update) | async-done | bytes 3276816 | tf_op jit(solution)/shard_map/all_gather | solution.py:24
  151.3 0.0 copy-done
  151.3 3.1 fusion.15
  154.4 0.2 copy.23
  154.6 138.5 %all-gather.3.cloned.1.call-done = bf16[2560,640]{1,0:T(8,128)(2,1)} async-done(((bf16[40,640]{1,0:T(8,128)(2,1)}), bf16[2560,640]{1,0:T(8,128)(2,1)}) %all-gather.3.cloned.1.call-update) | async-done | bytes 3276816 | tf_op jit(solution)/shard_map/all_gather | solution.py:23
  293.1 5.7 copy.21
  298.8 3.0 fusion.11
  301.8 4.2 select_reduce_fusion
  305.9 221.1 %pmax.7 = f32[8,512]{1,0:T(8,128)S(1)} all-reduce(f32[8,512]{1,0:T(8,128)S(1)} %get-tuple-element.9), channel_id=1, replica_groups=mesh['dp'=4,'head'=2,'tile'=64] {'tile'}, use_global_device_ids=true, to_apply=%region_1.2 | all-reduce | flops 4096 | bytes 32768 | tf_op jit(solution)/shard_map/pmax | solution.py:49
  527.0 5.7 bitcast_reduce_fusion
  532.7 219.7 %all-reduce = (f32[8,512]{1,0:T(8,128)S(1)}, f32[8,512]{1,0:T(8,128)S(1)}) all-reduce(f32[8,512]{1,0:T(8,128)S(1)} %get-tuple-element.6, f32[8,512]{1,0:T(8,128)S(1)} %get-tuple-element.5), channel_id=1, replica_groups=mesh['dp'=4,'head'=2,'tile'=64] {'tile'}, use_global_device_ids=true, to_apply=%region_5.6 | all-reduce | flops 8192 | bytes 65536 | tf_op jit(solution)/shard_map/psum | solution.py:51
  752.4 0.0 copy-start.1
  752.4 0.0 copy-start.3
  752.4 3.5 fusion.18
  755.8 0.0 copy-done.1
  755.9 1.2 copy-done.3
  757.1 0.0 copy-start.2
  757.1 1.6 fusion.21
  758.7 0.0 copy-start.4
  758.7 0.4 copy-done.2
  759.0 1.2 fusion.25
  760.3 0.4 copy-done.4
  760.7 2.4 fusion.4
  763.0 0.0 reduce-scatter.2.cloned.1.call-update
  763.1 132.3 %reduce-scatter.2.cloned.1.call-done = bf16[1,256,1280]{2,1,0:T(8,128)(2,1)} async-done(((bf16[1,256,2560]{2,1,0:T(8,128)(2,1)}), bf16[1,256,1280]{2,1,0:T(8,128)(2,1)}) %reduce-scatter.2.cloned.1.call-update) | async-done | bytes 655376 | tf_op jit(solution)/shard_map/reduce_scatter | solution.py:75
  (2 shorter events, 0.0 us)
Async XLA Ops:
  6.5 144.7 %copy-start = (bf16[1,256,2560]{2,1,0:T(8,128)(2,1)S(1)}, bf16[1,256,2560]{2,1,0:T(8,128)(2,1)}, u32[]{:S(2)}) copy-start(bf16[1,256,2560]{2,1,0:T(8,128)(2,1)} %param.7) | copy-start | bytes 3932164
  6.5 144.7 %all-gather.5.cloned.1.call-start = ((), (), s32[]{:S(2)}) async-start(), calls=%async_computation.2 | async-start | bytes 3328000 | tf_op jit(solution)/shard_map/all_gather | solution.py:24
  7.3 285.8 %all-gather.3.cloned.1.call-start = ((), (), s32[]{:S(2)}) async-start(), calls=%async_computation.1 | async-start | bytes 3328000 | tf_op jit(solution)/shard_map/all_gather | solution.py:23
  8.0 887.3 %reduce-scatter.2.cloned.1.call-start = ((), (), s32[]{:S(2)}) async-start(), calls=%async_computation.3 | async-start | bytes 1966080 | tf_op jit(solution)/shard_map/reduce_scatter | solution.py:75
  752.4 3.5 copy-start.1
  752.4 4.7 copy-start.3
  757.1 1.9 copy-start.2
  758.7 2.0 copy-start.4
Sparse Core Ops, SparseCore 0:
  10.3 140.9 all-gather.4
  154.2 138.8 all-gather.2
  763.2 132.0 reduce-scatter.1
where the time goes:
time: 902 us
  blocking collectives  441 us (49%)
  waiting for transfers between devices  411 us (46%)
  matrix products  24.5 us (3%)
  between operations  13.8 us (2%)
  local copies, waits for them, and re-layouts  10.6 us (1%)
    pmax x1, blocking collectives, per_device(): row_max = lax.pmax(local_max, 'tile')  221 us
    psum x1, blocking collectives, per_device(): lax.psum((jnp.sum(expd, axis=2), jnp.sum(expd * prob_grad, axis=2)), 'tile')  220 us
    all_gather x1, waiting for transfers between devices, per_device(): lax.all_gather(value_weight, 'tile', axis=0, tiled=True)  139 us
    all_gather x1, waiting for transfers between devices, per_device(): lax.all_gather(key_weight, 'tile', axis=0, tiled=True)  139 us
    reduce_scatter x1, waiting for transfers between devices, per_device(): lax.psum_scatter(rounded[None], 'head', scatter_dimension=2, tiled=True)  132 us
  transfers between devices with their start and end apart: 3, of which 3 were waited for; matrix products, arithmetic and copies ran while one was open for 1% of the time, Pallas kernels for 0%

commit v1 on v0

v1 whole, which is shorter than its diff:
```python
import jax
import jax.numpy as jnp
from jax import lax
from jax.sharding import Mesh
from jax.sharding import PartitionSpec as P

HDIM = 80
X_CHIPS = 4
NEG_LARGE = -1e30
SWAP = [(0, 1), (1, 0)]


def spread(value, axis, size):
    copies = jnp.broadcast_to(value[None], (size,) + value.shape)
    return lax.all_to_all(copies, axis, 0, 0, tiled=True)


def merge(stats, new_max):
    scale = jnp.exp(stats[:, 0] - new_max[None])
    return jnp.stack([new_max, jnp.sum(stats[:, 1] * scale, 0), jnp.sum(stats[:, 2] * scale, 0)])


def make_per_device(n_dp, n_zh, n_zl, n_x):
    def per_device(tiles_in, key_weight, value_weight, queries, out_grad, valid_count, tile_mask):
        inv_scale = HDIM ** (-0.5)
        tile_dev, width = tiles_in.shape[1:]
        latents, group = queries.shape
        rows = key_weight.shape[0]
        cols = group // n_x
        heads = cols // HDIM
        z = ("zh", "zl")
        core = lax.axis_index("head")
        plane = lax.axis_index("dp")
        mine = lax.axis_index("x")
        half = tile_dev // 2

        positions = (lax.axis_index(z) * n_x + mine) * tile_dev + jnp.arange(tile_dev, dtype=jnp.int32)
        kept = (tile_mask[0] == 1) | (positions == 0)
        valid = ((positions < valid_count[0]) & kept).astype(jnp.bfloat16)

        own_rows = lax.dynamic_slice(tiles_in[0], (core * half, 0), (half, width))
        own_tiles = lax.all_gather(own_rows, "x", axis=0, tiled=True)

        blocks = jnp.concatenate(
            [key_weight.reshape(rows, n_x, cols), value_weight.reshape(rows, n_x, cols)], axis=2
        ).transpose(1, 0, 2)
        flags = jnp.broadcast_to(
            jnp.pad(valid, (0, 2 * cols - tile_dev))[None, None], (n_x, 8, 2 * cols)
        )
        got = lax.all_to_all(jnp.concatenate([blocks, flags], axis=1), "x", 0, 0, tiled=True)
        flags = got[:, rows, :tile_dev]
        block = lax.dynamic_index_in_dim(got, plane, 0, keepdims=False)[:rows]
        plane_rows = lax.all_gather(block, z, axis=0, tiled=True)
        own_tiles, plane_rows = lax.optimization_barrier((own_tiles, plane_rows))
        other_tiles = lax.ppermute(own_tiles, "head", SWAP)
        weights = spread(plane_rows, "dp", n_dp)
        weights = weights.reshape(n_x, n_zh * n_zl, rows, 2 * cols).transpose(1, 0, 2, 3)
        weights = weights.reshape(width, 2 * cols)
        out_half = width // 2
        other_weights = lax.ppermute(
            lax.dynamic_slice(weights, ((1 - core) * out_half, 0), (out_half, 2 * cols)), "head", SWAP
        )
        own_weights = lax.dynamic_slice(weights, (core * out_half, 0), (out_half, 2 * cols))

        flags = flags.reshape(n_x, 2, half)
        order = jnp.stack([core, 1 - core])
        flags = jnp.take(flags, order, axis=1).transpose(1, 0, 2).reshape(-1)
        valid = (flags > 0.5)[None, :, None]

        tiles = jnp.concatenate([own_tiles, other_tiles], axis=0)
        tokens = tiles.shape[0]
        both = jnp.dot(tiles, weights, preferred_element_type=jnp.float32)
        keys = both[:, :cols].reshape(tokens, heads, HDIM)
        values = both[:, cols:].astype(jnp.bfloat16).reshape(tokens, heads, HDIM)
        query_heads = lax.dynamic_slice(queries, (0, mine * cols), (latents, cols)).reshape(latents, heads, HDIM)
        grad_heads = lax.dynamic_slice(out_grad[0], (0, mine * cols), (latents, cols)).reshape(latents, heads, HDIM)
        scores = (
            jnp.einsum(
                "thd,lhd->htl",
                keys,
                query_heads.astype(jnp.float32),
                precision=lax.Precision.HIGHEST,
                preferred_element_type=jnp.float32,
            )
            * inv_scale
        )
        prob_grad = jnp.einsum("thd,lhd->htl", values, grad_heads, preferred_element_type=jnp.float32)
        local_max = jnp.max(jnp.where(valid, scores, NEG_LARGE), axis=1)
        expd = jnp.where(valid, jnp.exp(scores - local_max[:, None]), 0.0)
        stats = jnp.stack([local_max, jnp.sum(expd, axis=1), jnp.sum(expd * prob_grad, axis=1)])
        for axis, size in (("zl", n_zl), ("zh", n_zh)):
            parts = spread(stats, axis, size)
            stats = merge(parts, jnp.max(parts[:, 0], axis=0))
        row_max, total, weighted = stats
        factor = jnp.exp(local_max - row_max) / total
        delta = weighted / total
        probs = expd * factor[:, None]
        dscore = (inv_scale * probs * (prob_grad - delta[:, None])).astype(jnp.bfloat16)
        value_grad = jnp.einsum(
            "htl,lhd->thd", probs.astype(jnp.bfloat16), grad_heads, preferred_element_type=jnp.float32
        )
        key_grad = jnp.einsum("htl,lhd->thd", dscore, query_heads, preferred_element_type=jnp.float32)
        grads = jnp.concatenate(
            [key_grad.reshape(tokens, cols), value_grad.reshape(tokens, cols)], axis=1
        ).astype(jnp.bfloat16)
        other_grads = lax.ppermute(grads, "head", SWAP)
        other_grads = jnp.concatenate([other_grads[tokens // 2 :], other_grads[: tokens // 2]], axis=0)
        dims = (((1,), (1,)), ((), ()))
        partial = lax.dot_general(grads, own_weights, dims, preferred_element_type=jnp.float32)
        partial = partial + lax.dot_general(other_grads, other_weights, dims, preferred_element_type=jnp.float32)
        partial = partial.astype(jnp.bfloat16).reshape(2, n_x, half, out_half).transpose(1, 0, 2, 3)
        parts = lax.all_to_all(partial, "x", 0, 0, tiled=True)
        summed = jnp.sum(parts.astype(jnp.float32), axis=0).astype(jnp.bfloat16)
        summed = jnp.where(core == 0, summed, summed[::-1])
        return summed.reshape(1, tile_dev, out_half)

    return per_device


def solution(mesh):
    n_dp, n_head, n_tile = mesh.devices.shape
    n_z = n_tile // X_CHIPS
    n_zl = 4
    fine = Mesh(
        mesh.devices.reshape(n_dp, n_head, n_z // n_zl, n_zl, X_CHIPS), ("dp", "head", "zh", "zl", "x")
    )
    tile = ("zh", "zl", "x")
    return jax.shard_map(
        make_per_device(n_dp, n_z // n_zl, n_zl, X_CHIPS),
        mesh=fine,
        in_specs=(
            P("dp", tile, None),
            P(tile, "head"),
            P(tile, "head"),
            P(None, "head"),
            P("dp", None, "head"),
            P("dp"),
            P("dp", tile),
        ),
        out_specs=P("dp", tile, "head"),
        check_vma=False,
    )
```

time: 902 us -> 207 us (0.23)
  blocking collectives: 441 us -> 40.7 us
  waiting for transfers between devices: 411 us -> 66.9 us
  starting transfers between devices: 0.08 us -> 35.6 us
    all_gather x2 -> x1, waiting for transfers between devices: 278 us -> 1.08 us  [per_device(): own_tiles = lax.all_gather(own_rows, 'x', axis=0, tiled=True)]
    pmax x1 -> x0, blocking collectives: 221 us -> none  [per_device(): row_max = lax.pmax(local_max, 'tile')]
    psum x1 -> x0, blocking collectives: 220 us -> none  [per_device(): lax.psum((jnp.sum(expd, axis=2), jnp.sum(expd * prob_grad, axis=2)), 'tile')]
    reduce_scatter x1 -> x0, waiting for transfers between devices: 132 us -> none  [per_device(): lax.psum_scatter(rounded[None], 'head', scatter_dimension=2, tiled=True)]
    all_to_all x0 -> x4, waiting for transfers between devices: none -> 65.8 us  [the longest x1 31.6 us: per_device(): parts = lax.all_to_all(partial, 'x', 0, 0, tiled=True)]
    all_gather x0 -> x1, blocking collectives: none -> 33.8 us  [per_device(): plane_rows = lax.all_gather(block, z, axis=0, tiled=True)]
    all_to_all x0 -> x4, starting transfers between devices: none -> 21.2 us  [the longest x2 11.8 us: spread(): return lax.all_to_all(copies, axis, 0, 0, tiled=True)]
    ppermute x0 -> x3, starting transfers between devices: none -> 14.4 us  [the longest x1 7.2 us: per_device(): other_tiles = lax.ppermute(own_tiles, 'head', SWAP)]
  transfers between devices with their start and end apart: 3 -> 8, of which waited for: 3 -> 5; matrix products, arithmetic and copies ran while one was open for 1% -> 9% of each run, Pallas kernels for 0% -> 0%
where the time goes in v1:
time: 207 us; the launch traced here: 206 us
  waiting for transfers between devices  66.9 us (32%)
  blocking collectives  40.7 us (20%)
  starting transfers between devices  35.6 us (17%)
  matrix products  23.7 us (11%)
  local copies, waits for them, and re-layouts  19.2 us (9%)
  between operations  14.4 us (7%)
  other arithmetic  6.06 us (3%)
    all_gather x1, blocking collectives, per_device(): plane_rows = lax.all_gather(block, z, axis=0, tiled=True)  33.8 us
    all_to_all x1, waiting for transfers between devices, per_device(): parts = lax.all_to_all(partial, 'x', 0, 0, tiled=True)  31.6 us
    all_to_all x2, waiting for transfers between devices, spread(): return lax.all_to_all(copies, axis, 0, 0, tiled=True)  29.3 us
    all_to_all x2, starting transfers between devices, spread(): return lax.all_to_all(copies, axis, 0, 0, tiled=True)  11.8 us
    ppermute x1, starting transfers between devices, per_device(): other_tiles = lax.ppermute(own_tiles, 'head', SWAP)  7.2 us
    all_to_all x1, blocking collectives, spread(): return lax.all_to_all(copies, axis, 0, 0, tiled=True)  6.91 us
    dot_general x1, matrix products, per_device(): both = jnp.dot(tiles, weights, preferred_element_type=jnp.float32)  5.16 us
    ppermute x1, starting transfers between devices, per_device(): other_grads = lax.ppermute(grads, 'head', SWAP)  5.15 us
  transfers between devices with their start and end apart: 8, of which 5 were waited for; matrix products, arithmetic and copies ran while one was open for 9% of the time, Pallas kernels for 0%

profile of v1, /device:TPU:1, one launch (start us, length us, event | category | flops | bytes accessed | tf_op | source)
XLA Modules:
  0.0 206.5 jit_solution(13320913288611016939)
XLA Ops:
  6.5 1.3 copy-done
  7.9 0.9 constant_dynamic-slice_fusion.3
  9.4 0.9 reshape.171
  10.4 0.9 reshape.172
  11.3 0.7 compare_reduce_fusion
  12.0 0.1 maximum_bitcast_fusion
  12.1 0.7 pad_maximum_fusion.1
  12.8 4.8 %all-to-all-start = ((bf16[4,48,320]{2,1,0:T(8,128)(2,1)}), bf16[4,48,320]{2,1,0:T(8,128)(2,1)S(1)}, u32[]{:S(2)}, u32[]{:S(2)}) async-start(bf16[4,48,320]{2,1,0:T(8,128)(2,1)} %pad_maximum_fusion.1), calls=%async_computation | async-start | bytes 294912 | tf_op jit(solution)/shard_map/all_to_all | solution.py:50
  17.6 4.9 %all-to-all-done = bf16[4,48,320]{2,1,0:T(8,128)(2,1)S(1)} async-done(((bf16[4,48,320]{2,1,0:T(8,128)(2,1)}), bf16[4,48,320]{2,1,0:T(8,128)(2,1)S(1)}, u32[]{:S(2)}, u32[]{:S(2)}) %all-to-all-start) | async-done | bytes 122912 | tf_op jit(solution)/shard_map/all_to_all | solution.py:50
  22.6 33.8 %all-gather.1 = bf16[1,640,320]{2,1,0:T(8,128)(2,1)S(1)} all-gather(bf16[1,40,320]{2,1,0:T(8,128)(2,1)S(1)} %constant_dynamic-slice_fusion.2), channel_id=3, replica_groups=mesh['dp'=4,'head'=2,'zh'=4,'zl'=4,'x'=4] {'zh','zl'}, dimensions={1}, use_global_device_ids=true | all-gather | bytes 435200 | tf_op jit(solution)/shard_map/all_gather | solution.py:53
  56.3 0.2 copy.74
  56.6 1.1 all-gather.4.cloned.1.call-done
  57.6 7.2 %collective-permute-start = (bf16[512,2560]{1,0:T(8,128)(2,1)}, bf16[512,2560]{1,0:T(8,128)(2,1)}, u32[]{:S(2)}, u32[]{:S(2)}) collective-permute-start(bf16[512,2560]{1,0:T(8,128)(2,1)} %bitcast.127), channel_id=1, source_target_pairs={{0,64},{64,0},{1,65},{65,1},{2,66},{66,2},{3,67},{67,3},{4,68},{68... | collective-permute-start | bytes 7864328 | tf_op jit(solution)/shard_map/ppermute | solution.py:55
  64.9 1.3 broadcast_in_dim.62
  66.2 4.4 %all-to-all-start.1 = ((bf16[4,640,320]{1,2,0:T(8,128)(2,1)}), bf16[4,640,320]{1,2,0:T(8,128)(2,1)}, u32[]{:S(2)}, u32[]{:S(2)}) async-start(bf16[4,640,320]{1,2,0:T(8,128)(2,1)} %broadcast_in_dim.62), calls=%async_computation.1 | async-start | bytes 3276800 | tf_op jit(solution)/shard_map/all_to_all | solution.py:15
  70.6 1.1 constant_dynamic-slice_fusion.4
  71.7 0.1 copy.70
  71.8 1.1 constant_dynamic-slice_fusion.1
  73.0 0.8 copy.77
  73.8 0.1 fusion.25
  73.8 0.1 compare_and_fusion
  73.9 0.6 gather_fusion
  74.5 0.1 select_compare_fusion
  74.6 17.4 %all-to-all-done.1 = bf16[4,640,320]{1,2,0:T(8,128)(2,1)} async-done(((bf16[4,640,320]{1,2,0:T(8,128)(2,1)}), bf16[4,640,320]{1,2,0:T(8,128)(2,1)}, u32[]{:S(2)}, u32[]{:S(2)}) %all-to-all-start.1) | async-done | bytes 1638432 | tf_op jit(solution)/shard_map/all_to_all | solution.py:15
  92.0 2.7 %copy.75 = bf16[4,640,320]{2,1,0:T(8,128)(2,1)S(1)} copy(bf16[4,640,320]{1,2,0:T(8,128)(2,1)} %all-to-all-done.1) | data formatting | bytes 3276800 | tf_op jit(solution)/shard_map/all_to_all | solution.py:15
  94.8 0.2 copy.76
  95.0 5.2 %fusion = f32[1024,320]{0,1:T(8,128)S(1)} fusion(bf16[2560,320]{1,0:T(8,128)(2,1)S(1)} %bitcast.102, bf16[512,2560]{1,0:T(8,128)(2,1)} %collective-permute-done, bf16[512,2560]{1,0:T(8,128)(2,1)} %bitcast.128), kind=kOutput, calls=%fused_computation.1 | convolution fusion | flops 1688207360 | bytes 8192000 | tf_op jit(solution)/shard_map/dot_general | solution.py:72
  100.3 2.3 %select_reduce_fusion = (f32[2,512]{1,0:T(2,128)S(1)}, f32[2,1024,512]{2,1,0:T(8,128)S(1)}) fusion(pred[1024]{0:T(1024)(128)(4,1)S(1)} %bitcast.122, f32[1024,2,80]{0,2,1:T(8,128)S(1)} %bitcast.105, bf16[512,2,80]{0,2,1:T(8,128)(2,1)S(1)} %bitcast.112), kind=kOutput, calls=%fused_computation.9 | convolution fusion | flops 1009777664 | bytes 5018624 | tf_op jit(solution)/shard_map/thd,lhd->htl/dot_general | solution.py:78
  102.5 3.2 %fusion.29 = (f32[2,512]{1,0:T(2,128)S(1)}, f32[2,512]{1,0:T(2,128)S(1)}, f32[2,1024,512]{2,1,0:T(8,128)}) fusion(f32[2,512]{1,0:T(2,128)S(1)} %get-tuple-element.19, f32[2,1024,512]{2,1,0:T(8,128)S(1)} %get-tuple-element.20, pred[1024]{0:T(1024)(128)(4,1)S(1)} %bitcast.123, bf16[1024,2,80]{0,2,1:T(8,128)(2,1)S(1)} %bitcast.111, ...), kind=kOutput, calls=%fused_computation.67 | convolution fusion | flops 174061568 | bytes 8893440 | tf_op jit(solution)/shard_map/thd,lhd->htl/dot_general | solution.py:87
  105.8 6.9 %all_to_all.25 = f32[4,3,2,512]{3,2,1,0:T(2,128)S(1)} all-to-all(f32[4,3,2,512]{3,2,1,0:T(2,128)S(1)} %broadcast_in_dim.65), channel_id=1, replica_groups=mesh['dp'=4,'head'=2,'zh'=4,'zl'=4,'x'=4] {'zl'}, dimensions={0} | all-to-all | bytes 98304 | tf_op jit(solution)/shard_map/all_to_all | solution.py:15
  112.8 0.6 broadcast_in_dim.66
  113.4 7.4 %all-to-all-start.3 = ((f32[4,3,2,512]{3,2,1,0:T(2,128)}), f32[4,3,2,512]{3,2,1,0:T(2,128)S(1)}, u32[]{:S(2)}, u32[]{:S(2)}) async-start(f32[4,3,2,512]{3,2,1,0:T(2,128)} %broadcast_in_dim.66), calls=%async_computation.3 | async-start | bytes 98304 | tf_op jit(solution)/shard_map/all_to_all | solution.py:15
  120.8 11.9 %all-to-all-done.3 = f32[4,3,2,512]{3,2,1,0:T(2,128)S(1)} async-done(((f32[4,3,2,512]{3,2,1,0:T(2,128)}), f32[4,3,2,512]{3,2,1,0:T(2,128)S(1)}, u32[]{:S(2)}, u32[]{:S(2)}) %all-to-all-start.3) | async-done | bytes 49184 | tf_op jit(solution)/shard_map/all_to_all | solution.py:15
  132.8 3.5 %fusion.8 = bf16[2,80,1024]{2,1,0:T(8,128)(2,1)S(1)} fusion(bf16[512,2,80]{0,2,1:T(8,128)(2,1)S(1)} %bitcast.115, f32[2,512]{1,0:T(2,128)S(1)} %get-tuple-element.18, f32[2,1024,512]{2,1,0:T(8,128)} %copy-done.1, f32[2,512]{1,0:T(2,128)S(1)} %get-tuple-element.19, pred[1024]{0:T(1024)(128)(4,1)S(1)} %bitcast.124), kind=kOutput, calls=%fused_computation.16 | convolution fusion | flops 173178880 | bytes 4695040 | tf_op jit(solution)/shard_map/htl,lhd->thd/dot_general | solution.py:99
  136.4 4.1 %fusion.7 = bf16[2,80,1024]{2,1,0:T(8,128)(2,1)S(1)} fusion(bf16[512,2,80]{0,2,1:T(8,128)(2,1)S(1)} %bitcast.113, f32[2,1024,512]{2,1,0:T(8,128)} %get-tuple-element.21, f32[2,512]{1,0:T(2,128)S(1)} %get-tuple-element.17, f32[2,512]{1,0:T(2,128)S(1)} %get-tuple-element.18, f32[2,1024,512]{2,1,0:T(8,128)S(1)} %copy-done.2, ...), kind=kOutput, calls=%fused_computation.15 | convolution fusion | flops 176324608 | bytes 8893440 | tf_op jit(solution)/shard_map/htl,lhd->thd/dot_general | solution.py:102
  140.5 0.9 pad_maximum_fusion
  141.4 5.1 %collective-permute-start.1 = (bf16[1024,320]{0,1:T(8,128)(2,1)}, bf16[1024,320]{0,1:T(8,128)(2,1)}, u32[]{:S(2)}, u32[]{:S(2)}) collective-permute-start(bf16[1024,320]{0,1:T(8,128)(2,1)} %pad_maximum_fusion), channel_id=1, source_target_pairs={{0,64},{64,0},{1,65},{65,1},{2,66},{66,2},{3,67},{67,3},{4,68},{68... | collective-permute-start | bytes 1966088 | tf_op jit(solution)/shard_map/ppermute | solution.py:106
  146.6 1.1 constant_dynamic-slice_fusion
  147.6 2.2 %copy.88 = bf16[1280,320]{0,1:T(8,128)(2,1)} copy(bf16[1280,320]{1,0:T(8,128)(2,1)} %constant_dynamic-slice_fusion) | data formatting | bytes 1638400 | tf_op jit(solution)/shard_map/dynamic_slice | solution.py:61
  149.8 2.1 %collective-permute-start.2 = (bf16[1280,320]{0,1:T(8,128)(2,1)}, bf16[1280,320]{0,1:T(8,128)(2,1)}, u32[]{:S(2)}, u32[]{:S(2)}) collective-permute-start(bf16[1280,320]{0,1:T(8,128)(2,1)} %copy.88), channel_id=1, source_target_pairs={{0,64},{64,0},{1,65},{65,1},{2,66},{66,2},{3,67},{67,3},{4,68},{68... | collective-permute-start | bytes 2457608 | tf_op jit(solution)/shard_map/ppermute | solution.py:60
  151.9 2.6 %fusion.9 = f32[1024,1280]{1,0:T(8,128)S(1)} fusion(bf16[2560,320]{1,0:T(8,128)(2,1)S(1)} %bitcast.104, s32[]{:T(128)S(6)} %select_n.63, bf16[1024,160]{0,1:T(8,128)(2,1)} %bitcast.108, bf16[1024,160]{0,1:T(8,128)(2,1)} %bitcast.110), kind=kOutput, calls=%fused_computation.18 | convolution fusion | flops 840171520 | bytes 6881284 | tf_op jit(solution)/shard_map/dot_general | solution.py:109
  154.6 1.1 fusion.30
  155.7 2.8 %add_convert_fusion = bf16[1024,1280]{1,0:T(8,128)(2,1)S(1)} fusion(f32[1024,1280]{1,0:T(8,128)S(1)} %fusion.9, bf16[1280,320]{0,1:T(8,128)(2,1)} %collective-permute-done.2, bf16[512,320]{0,1:T(8,128)(2,1)S(1)} %get-tuple-element.16, bf16[512,320]{0,1:T(8,128)(2,1)S(1)} %get-tuple-element.15), kind=kOutput, calls=%fused_computation.5 | convolution fusion | flops 842792960 | bytes 9338880 | tf_op jit(solution)/shard_map/dot_general | solution.py:110
  158.5 1.7 copy.102
  160.2 4.5 %all-to-all-start.4 = ((bf16[4,2,128,1280]{3,2,1,0:T(8,128)(2,1)}), bf16[4,2,128,1280]{3,2,1,0:T(8,128)(2,1)}, u32[]{:S(2)}, u32[]{:S(2)}) async-start(bf16[4,2,128,1280]{3,2,1,0:T(8,128)(2,1)} %bitcast.99), calls=%async_computation.4 | async-start | bytes 5242880 | tf_op jit(solution)/shard_map/all_to_all | solution.py:112
  164.8 31.6 %all-to-all-done.4 = bf16[4,2,128,1280]{3,2,1,0:T(8,128)(2,1)} async-done(((bf16[4,2,128,1280]{3,2,1,0:T(8,128)(2,1)}), bf16[4,2,128,1280]{3,2,1,0:T(8,128)(2,1)}, u32[]{:S(2)}, u32[]{:S(2)}) %all-to-all-start.4) | async-done | bytes 2621472 | tf_op jit(solution)/shard_map/all_to_all | solution.py:112
  196.4 2.3 %reduce_sum.72 = bf16[2,128,1280]{2,1,0:T(8,128)(2,1)S(1)} reduce(bf16[4,2,128,1280]{3,2,1,0:T(8,128)(2,1)} %all-to-all-done.4, bf16[]{:T(256)} %constant.75.clone.1), dimensions={0}, to_apply=%region_9.10 | reduce | flops 983040 | bytes 3276802 | tf_op jit(solution)/shard_map/reduce_sum | solution.py:113
  198.7 0.9 reverse_select_fusion
  (39 shorter events, 0.4 us)
Async XLA Ops:
  6.5 1.3 copy-start
  6.5 51.1 %all-gather.4.cloned.1.call-start = ((), (), s32[]{:S(2)}) async-start(), calls=%async_computation.5 | async-start | bytes 3276800 | tf_op jit(solution)/shard_map/all_gather | solution.py:42
  12.8 9.8 %all-to-all-start = ((bf16[4,48,320]{2,1,0:T(8,128)(2,1)}), bf16[4,48,320]{2,1,0:T(8,128)(2,1)S(1)}, u32[]{:S(2)}, u32[]{:S(2)}) async-start(bf16[4,48,320]{2,1,0:T(8,128)(2,1)} %pad_maximum_fusion.1), calls=%async_computation | async-start | bytes 294912 | tf_op jit(solution)/shard_map/all_to_all | solution.py:50
  57.6 37.3 %collective-permute-start = (bf16[512,2560]{1,0:T(8,128)(2,1)}, bf16[512,2560]{1,0:T(8,128)(2,1)}, u32[]{:S(2)}, u32[]{:S(2)}) collective-permute-start(bf16[512,2560]{1,0:T(8,128)(2,1)} %bitcast.127), channel_id=1, source_target_pairs={{0,64},{64,0},{1,65},{65,1},{2,66},{66,2},{3,67},{67,3},{4,68},{68... | collective-permute-start | bytes 7864328 | tf_op jit(solution)/shard_map/ppermute | solution.py:55
  66.2 25.9 %all-to-all-start.1 = ((bf16[4,640,320]{1,2,0:T(8,128)(2,1)}), bf16[4,640,320]{1,2,0:T(8,128)(2,1)}, u32[]{:S(2)}, u32[]{:S(2)}) async-start(bf16[4,640,320]{1,2,0:T(8,128)(2,1)} %broadcast_in_dim.62), calls=%async_computation.1 | async-start | bytes 3276800 | tf_op jit(solution)/shard_map/all_to_all | solution.py:15
  95.0 5.2 %copy-start.3 = (bf16[16,4,40,320]{3,2,1,0:T(8,128)(2,1)}, bf16[16,4,40,320]{3,2,1,0:T(8,128)(2,1)S(1)}, u32[]{:S(2)}) copy-start(bf16[16,4,40,320]{3,2,1,0:T(8,128)(2,1)S(1)} %copy.76) | copy-start | bytes 4915204
  100.2 2.4 %copy-start.7 = (bf16[1,512,160]{1,2,0:T(8,128)(2,1)S(1)}, bf16[1,512,160]{1,2,0:T(8,128)(2,1)}, u32[]{:S(2)}) copy-start(bf16[1,512,160]{1,2,0:T(8,128)(2,1)} %copy.77) | copy-start | bytes 491524
  102.5 3.2 %copy-start.1 = (f32[2,1024,512]{2,1,0:T(8,128)}, f32[2,1024,512]{2,1,0:T(8,128)S(1)}, u32[]{:S(2)}) copy-start(f32[2,1024,512]{2,1,0:T(8,128)S(1)} %get-tuple-element.20) | copy-start | bytes 12582916
  113.4 19.3 %all-to-all-start.3 = ((f32[4,3,2,512]{3,2,1,0:T(2,128)}), f32[4,3,2,512]{3,2,1,0:T(2,128)S(1)}, u32[]{:S(2)}, u32[]{:S(2)}) async-start(f32[4,3,2,512]{3,2,1,0:T(2,128)} %broadcast_in_dim.66), calls=%async_computation.3 | async-start | bytes 98304 | tf_op jit(solution)/shard_map/all_to_all | solution.py:15
  132.7 3.6 %copy-start.2 = (f32[2,1024,512]{2,1,0:T(8,128)S(1)}, f32[2,1024,512]{2,1,0:T(8,128)}, u32[]{:S(2)}) copy-start(f32[2,1024,512]{2,1,0:T(8,128)} %copy-done.1) | copy-start | bytes 12582916
  136.3 4.1 %copy-start.5 = (bf16[2,80,1024]{2,1,0:T(8,128)(2,1)}, bf16[2,80,1024]{2,1,0:T(8,128)(2,1)S(1)}, u32[]{:S(2)}) copy-start(bf16[2,80,1024]{2,1,0:T(8,128)(2,1)S(1)} %fusion.8) | copy-start | bytes 983044
  136.3 10.2 %copy-start.4 = (bf16[16,4,40,320]{3,2,1,0:T(8,128)(2,1)S(1)}, bf16[16,4,40,320]{3,2,1,0:T(8,128)(2,1)}, u32[]{:S(2)}) copy-start(bf16[16,4,40,320]{3,2,1,0:T(8,128)(2,1)} %copy-done.3) | copy-start | bytes 4915204
  140.4 1.0 copy-start.6
  141.4 13.2 %collective-permute-start.1 = (bf16[1024,320]{0,1:T(8,128)(2,1)}, bf16[1024,320]{0,1:T(8,128)(2,1)}, u32[]{:S(2)}, u32[]{:S(2)}) collective-permute-start(bf16[1024,320]{0,1:T(8,128)(2,1)} %pad_maximum_fusion), channel_id=1, source_target_pairs={{0,64},{64,0},{1,65},{65,1},{2,66},{66,2},{3,67},{67,3},{4,68},{68... | collective-permute-start | bytes 1966088 | tf_op jit(solution)/shard_map/ppermute | solution.py:106
  149.8 5.9 %collective-permute-start.2 = (bf16[1280,320]{0,1:T(8,128)(2,1)}, bf16[1280,320]{0,1:T(8,128)(2,1)}, u32[]{:S(2)}, u32[]{:S(2)}) collective-permute-start(bf16[1280,320]{0,1:T(8,128)(2,1)} %copy.88), channel_id=1, source_target_pairs={{0,64},{64,0},{1,65},{65,1},{2,66},{66,2},{3,67},{67,3},{4,68},{68... | collective-permute-start | bytes 2457608 | tf_op jit(solution)/shard_map/ppermute | solution.py:60
  160.2 36.2 %all-to-all-start.4 = ((bf16[4,2,128,1280]{3,2,1,0:T(8,128)(2,1)}), bf16[4,2,128,1280]{3,2,1,0:T(8,128)(2,1)}, u32[]{:S(2)}, u32[]{:S(2)}) async-start(bf16[4,2,128,1280]{3,2,1,0:T(8,128)(2,1)} %bitcast.99), calls=%async_computation.4 | async-start | bytes 5242880 | tf_op jit(solution)/shard_map/all_to_all | solution.py:112
Sparse Core Ops, SparseCore 0:
  9.5 48.1 all-gather.3
